TPU v7x, 32 devices: a whole 2x2x4 slice. The times are simulated.
32 devices in a mesh: seq: 4 (over x, core), chan: 8 (over z, y).
Axes of the slice: x: 2, y: 2, z: 4, core: 2. Of those that a mesh axis runs over, the one named last changes fastest.
Arguments:
- features: bfloat16 [3, 4096, 512], P(None, 'chan', 'seq'), may hold values from -6 to 6
- cotangent: bfloat16 [4096, 512], P('chan', 'seq'), may hold values from -6 to 6
- long_filter: bfloat16 [4096, 512], P('chan', 'seq'), may hold values from -0.25 to 0.25
- short_filters: float32 [3, 4096, 3], P(None, 'chan'), may hold values from -3.5 to 3.5
- skip_gain: float32 [4096], P('chan'), may hold values from -4 to 4
Outputs:
- gated_out: bfloat16 [4096, 512], P('chan', 'seq')
- feature_grad: bfloat16 [3, 4096, 512], P(None, 'chan', 'seq')
- long_grad: bfloat16 [4096, 512], P('chan', 'seq')
- short_grad: float32 [3, 4096, 3], P(None, 'chan')
- skip_grad: float32 [4096], P('chan')
All inputs are finite; a program needn't handle non-finite values.
Results may differ from a plain program's by a relative error of at most 0.015.
Values may be sent and summed in bfloat16 or wider, within the bound.
A program may use at most 64 MiB of HBM per device.

v0:
```python
import math
import jax
import jax.numpy as jnp
from jax import lax
from jax.sharding import PartitionSpec as P

inner_length = 128
radix_width = 8


def phase_tables(row_count, col_count, length, direction):
    phase_index = (
        lax.iota(jnp.int32, row_count)[:, None] * lax.iota(jnp.int32, col_count)[None, :] % length
    )
    angles = direction * 2.0 * math.pi / length * phase_index.astype(jnp.float32)
    return (jnp.cos(angles), jnp.sin(angles))


def last_axis(operand, matrix):
    return jnp.einsum("...n,nk->...k", operand, matrix, precision=lax.Precision.HIGH)


def first_axis(operand, matrix):
    return jnp.einsum("...ab,ak->...kb", operand, matrix, precision=lax.Precision.HIGH)


def transform(real_part, imag_part, direction):
    length = real_part.shape[-1]
    if length <= inner_length or length % radix_width != 0:
        cos_table, sin_table = phase_tables(length, length, length, direction)
        return (
            last_axis(real_part, cos_table) - last_axis(imag_part, sin_table),
            last_axis(real_part, sin_table) + last_axis(imag_part, cos_table),
        )
    rest_length = length // radix_width
    grid_shape = real_part.shape[:-1] + (radix_width, rest_length)
    real_grid = real_part.reshape(grid_shape)
    imag_grid = imag_part.reshape(grid_shape)
    cos_table, sin_table = phase_tables(radix_width, radix_width, radix_width, direction)
    section_real = first_axis(real_grid, cos_table) - first_axis(imag_grid, sin_table)
    section_imag = first_axis(real_grid, sin_table) + first_axis(imag_grid, cos_table)
    twist_cos, twist_sin = phase_tables(radix_width, rest_length, length, direction)
    turned_real = section_real * twist_cos - section_imag * twist_sin
    turned_imag = section_real * twist_sin + section_imag * twist_cos
    inner_real, inner_imag = transform(turned_real, turned_imag, direction)
    return (
        jnp.swapaxes(inner_real, -1, -2).reshape(real_part.shape),
        jnp.swapaxes(inner_imag, -1, -2).reshape(real_part.shape),
    )


def spectral(mixed_term, gated_grad, kernel, local_gain):
    length = mixed_term.shape[-1]
    mixed_wide = mixed_term.astype(jnp.float32)
    gated_wide = gated_grad.astype(jnp.float32)
    kernel_wide = kernel.astype(jnp.float32)
    extend = ((0, 0), (0, length))
    real_in = jnp.stack([jnp.pad(mixed_wide, extend), jnp.pad(kernel_wide, extend)])
    imag_in = jnp.stack(
        [jnp.pad(gated_wide, extend), jnp.zeros((kernel_wide.shape[0], 2 * length), jnp.float32)]
    )
    freq_real, freq_imag = transform(real_in, imag_in, -1.0)
    packed_real = freq_real[0]
    packed_imag = freq_imag[0]
    mirror_real = jnp.roll(jnp.flip(packed_real, -1), 1, -1)
    mirror_imag = jnp.roll(jnp.flip(packed_imag, -1), 1, -1)
    mix_real = 0.5 * (packed_real + mirror_real)
    mix_imag = 0.5 * (packed_imag - mirror_imag)
    grad_real = 0.5 * (packed_imag + mirror_imag)
    grad_imag = 0.5 * (mirror_real - packed_real)
    kern_real = freq_real[1]
    kern_imag = freq_imag[1]
    conv_real = mix_real * kern_real - mix_imag * kern_imag
    conv_imag = mix_real * kern_imag + mix_imag * kern_real
    corr_real = grad_real * kern_real + grad_imag * kern_imag
    corr_imag = grad_imag * kern_real - grad_real * kern_imag
    cross_real = grad_real * mix_real + grad_imag * mix_imag
    cross_imag = grad_imag * mix_real - grad_real * mix_imag
    back_real = jnp.stack([conv_real - corr_imag, cross_real])
    back_imag = jnp.stack([conv_imag + corr_real, cross_imag])
    time_real, time_imag = transform(back_real, back_imag, 1.0)
    inverse_scale = 1.0 / (2 * length)
    conv_part = time_real[0, :, :length] * inverse_scale
    corr_part = time_imag[0, :, :length] * inverse_scale
    cross_part = time_real[1, :, :length] * inverse_scale
    gain_column = local_gain[:, None]
    long_out = (conv_part + gain_column * mixed_wide).astype(jnp.bfloat16)
    mixed_grad = (corr_part + gain_column * gated_wide).astype(jnp.bfloat16)
    return (long_out, mixed_grad, cross_part.astype(jnp.bfloat16))


def featurize(history, weights, margin, span_count):
    running = weights[:, :, 0:1] * history[:, :, margin : margin + span_count]
    for offset in range(1, margin + 1):
        running = (
            running
            + weights[:, :, offset : offset + 1]
            * history[:, :, margin - offset : margin - offset + span_count]
        )
    return running


def unfeaturize(padded_grad, weights, span_count):
    running = weights[:, :, 0:1] * padded_grad[:, :, 0:span_count]
    for offset in range(1, weights.shape[2]):
        running = (
            running
            + weights[:, :, offset : offset + 1] * padded_grad[:, :, offset : offset + span_count]
        )
    return running


def tap_grads(primed_grad, history, margin, span_count):
    columns = []
    for offset in range(margin + 1):
        columns.append(
            jnp.sum(
                primed_grad * history[:, :, margin - offset : margin - offset + span_count], axis=-1
            )
        )
    return jnp.stack(columns, axis=-1)


def shards(features, cotangent, long_filter, short_filters, skip_gain):
    groups = lax.axis_size("seq")
    seq_index = lax.axis_index("seq")
    channels = features.shape[1]
    per_group = channels // groups
    margin = short_filters.shape[2] - 1
    local_gain = lax.dynamic_slice_in_dim(skip_gain, seq_index * per_group, per_group, 0)
    stacked = jnp.concatenate([features, cotangent[None], long_filter[None]], 0)
    columns = lax.all_to_all(stacked, "seq", split_axis=1, concat_axis=2, tiled=True)
    weights = lax.dynamic_slice_in_dim(short_filters, seq_index * per_group, per_group, 1)
    length = columns.shape[2]
    history = jnp.pad(columns[:3].astype(jnp.float32), ((0, 0), (0, 0), (margin, 0)))
    primed = featurize(history, weights, margin, length)
    mixed_term = (primed[1] * primed[2]).astype(jnp.bfloat16)
    cot_wide = columns[3].astype(jnp.float32)
    gated_grad = (cot_wide * primed[0]).astype(jnp.bfloat16)
    long_out, mixed_grad, kernel_grad = spectral(mixed_term, gated_grad, columns[4], local_gain)
    long_wide = long_out.astype(jnp.float32)
    mixed_back = mixed_grad.astype(jnp.float32)
    gated_out = (primed[0] * long_wide).astype(jnp.bfloat16)
    primed_grad = jnp.stack([cot_wide * long_wide, mixed_back * primed[2], mixed_back * primed[1]])
    padded_grad = jnp.pad(primed_grad, ((0, 0), (0, 0), (0, margin)))
    feature_grad = unfeaturize(padded_grad, weights, length).astype(jnp.bfloat16)
    taps_grad = tap_grads(primed_grad, history, margin, length)
    gain_grad = jnp.sum(gated_grad.astype(jnp.float32) * mixed_term.astype(jnp.float32), axis=-1)
    results = jnp.concatenate([gated_out[None], feature_grad, kernel_grad[None]], 0)
    row_blocks = lax.all_to_all(results, "seq", split_axis=2, concat_axis=1, tiled=True)
    short_grad, skip_grad = (
        lax.all_gather(taps_grad, "seq", axis=1, tiled=True),
        lax.all_gather(gain_grad, "seq", axis=0, tiled=True),
    )
    return (row_blocks[0], row_blocks[1:4], row_blocks[4], short_grad, skip_grad)


def solution(mesh):
    placed = (
        P(None, "chan", "seq"),
        P("chan", "seq"),
        P("chan", "seq"),
        P(None, "chan", None),
        P("chan"),
    )
    return jax.shard_map(
        shards,
        mesh=mesh,
        in_specs=placed,
        out_specs=(
            P("chan", "seq"),
            P(None, "chan", "seq"),
            P("chan", "seq"),
            P(None, "chan", None),
            P("chan"),
        ),
        check_vma=False,
    )
```

profile of v0, /device:TPU:0, one launch (start us, length us, event | category | flops | bytes accessed | tf_op | source)
XLA Modules:
  0.0 104.6 jit_solution(2643128398959037245)
XLA Ops:
  0.6 1.2 %copy.108 = bf16[1,512,128]{2,0,1:T(2,128)(2,1)S(1)} copy(bf16[1,512,128]{2,1,0:T(8,128)(2,1)} %bitcast.192) | data formatting | bytes 262144 | tf_op jit(solution)/shard_map/broadcast_in_dim | solution.py:131
  1.8 1.1 %copy.107 = bf16[1,512,128]{2,0,1:T(2,128)(2,1)S(1)} copy(bf16[1,512,128]{2,1,0:T(8,128)(2,1)} %bitcast.193) | data formatting | bytes 262144 | tf_op jit(solution)/shard_map/broadcast_in_dim | solution.py:131
  2.9 0.3 copy.106
  3.3 1.9 %pad_maximum_fusion = bf16[5,512,128]{2,0,1:T(8,128)(2,1)} fusion(bf16[1,512,128]{2,0,1:T(2,128)(2,1)S(1)} %copy.108, bf16[1,512,128]{2,0,1:T(2,128)(2,1)S(1)} %copy.107, bf16[3,512,128]{2,0,1:T(4,128)(2,1)S(1)} %copy.106), kind=kLoop, calls=%fused_computation.12 | loop fusion | flops 1966080 | bytes 1310720 | tf_op jit(solution)/shard_map/concatenate | solution.py:131
  5.1 4.2 %all-to-all-start = ((bf16[5,512,128]{2,0,1:T(8,128)(2,1)}), bf16[5,512,128]{2,0,1:T(8,128)(2,1)S(1)}, u32[]{:S(2)}, u32[]{:S(2)}) async-start(bf16[5,512,128]{2,0,1:T(8,128)(2,1)} %pad_maximum_fusion), calls=%async_computation | async-start | bytes 2097152 | tf_op jit(solution)/shard_map/all_to_all | solution.py:132
  9.4 0.9 constant_dynamic-slice_fusion.1
  10.3 1.3 %dynamic_slice.7 = f32[128]{0:T(128)} dynamic-slice(f32[512]{0:T(512)} %param.9, s32[]{:T(128)S(6)} %select_n.84), dynamic_slice_sizes={128} | dynamic-slice | bytes 1028 | tf_op jit(solution)/shard_map/dynamic_slice | solution.py:130
  11.6 0.7 multiply_sine_fusion.7
  12.3 0.6 multiply_sine_fusion.6
  12.9 10.9 %all-to-all-done = bf16[5,512,128]{2,0,1:T(8,128)(2,1)S(1)} async-done(((bf16[5,512,128]{2,0,1:T(8,128)(2,1)}), bf16[5,512,128]{2,0,1:T(8,128)(2,1)S(1)}, u32[]{:S(2)}, u32[]{:S(2)}) %all-to-all-start) | async-done | bytes 655392 | tf_op jit(solution)/shard_map/all_to_all | solution.py:132
  23.8 0.7 copy.109
  24.7 0.6 copy-done.1
  25.7 1.3 %multiply_reduce_fusion.2 = (f32[128]{0:T(128)}, f32[128,512]{0,1:T(8,128)}, bf16[1,128,512]{1,2,0:T(8,128)(2,1)S(1)}) fusion(f32[3,128,512]{1,2,0:T(8,128)S(1)} %multiply_add_fusion, f32[1,128,4,128]{1,3,2,0:T(8,128)S(1)} %get-tuple-element.51), kind=kLoop, calls=%fused_computation.80 | loop fusion | flops 524160 | bytes 1442304 | tf_op jit(solution)/shard_map/reduce_sum | solution.py:148
  27.3 1.6 %fusion.18 = f32[8,2,128,128]{3,0,2,1:T(8,128)} fusion(f32[1,128,8,128]{3,2,1,0:T(8,128)S(1)} %bitcast.169, f32[1,128,8,128]{3,2,1,0:T(8,128)S(1)} %copy.156), kind=kOutput, calls=%fused_computation.36 | convolution fusion | flops 12845952 | bytes 2097152 | tf_op jit(solution)/shard_map/...ab,ak->...kb/dot_general | solution.py:24
  28.9 1.6 %fusion.19 = f32[8,2,128,128]{3,0,2,1:T(8,128)} fusion(f32[1,128,8,128]{3,2,1,0:T(8,128)S(1)} %bitcast.170, f32[1,128,8,128]{3,2,1,0:T(8,128)S(1)} %copy.156), kind=kOutput, calls=%fused_computation.37 | convolution fusion | flops 12845952 | bytes 2097152 | tf_op jit(solution)/shard_map/...ab,ak->...kb/dot_general | solution.py:24
  30.5 1.1 %stack.58 = f32[2,128,1024]{1,2,0:T(8,128)} pad(f32[1,128,1024]{1,2,0:T(8,128)S(1)} %pad_bitcast_fusion, f32[]{:T(128)} %constant.67.clone.1), padding=0_1x0_0x0_0 | pad | bytes 1572868 | tf_op jit(solution)/shard_map/stack | solution.py:59
  31.6 1.6 %copy.158 = f32[2,128,8,128]{3,2,1,0:T(8,128)S(1)} copy(f32[2,128,8,128]{1,3,2,0:T(8,128)} %bitcast.176) | data formatting | bytes 2097152 | tf_op jit(solution)/shard_map/reshape | solution.py:38
  33.2 1.9 %convolution_add_fusion.3 = f32[8,2,128,128]{3,0,2,1:T(8,128)S(1)} fusion(f32[8,2,128,128]{3,0,2,1:T(8,128)} %fusion.18, f32[2,128,8,128]{3,2,1,0:T(8,128)S(1)} %copy.158), kind=kOutput, calls=%fused_computation.10 | convolution fusion | flops 12845952 | bytes 3145728 | tf_op jit(solution)/shard_map/...ab,ak->...kb/dot_general | solution.py:24
  35.2 0.8 add_bitcast_fusion.1
  36.0 0.9 fusion.12
  36.9 0.9 fusion.14
  37.8 0.9 fusion.3
  38.6 0.9 fusion.168
  39.5 0.3 copy.194
  39.8 0.9 slice.152
  40.7 0.5 slice_bitcast_fusion.1
  41.2 0.9 fusion.2
  42.2 0.3 copy.193
  42.5 0.8 slice.156
  43.3 0.5 slice_bitcast_fusion
  43.8 1.1 %copy.127 = f32[1,128,128,8]{1,3,2,0:T(8,128)} copy(f32[1,128,128,8]{1,2,3,0:T(8,128)S(1)} %get-tuple-element.45) | data formatting | bytes 1048576 | tf_op jit(solution)/shard_map/slice | solution.py:72
  44.9 1.3 %copy.128 = f32[1,128,8,128]{3,2,1,0:T(8,128)S(1)} copy(f32[1,128,8,128]{1,3,2,0:T(8,128)} %bitcast.187) | data formatting | bytes 1048576 | tf_op jit(solution)/shard_map/squeeze | solution.py:72
  46.2 2.2 %copy.119 = f32[1,128,128,8]{1,3,2,0:T(8,128)} copy(f32[1,128,128,8]{1,2,3,0:T(8,128)} %get-tuple-element.47) | data formatting | bytes 1048576 | tf_op jit(solution)/shard_map/slice | solution.py:71
  48.4 2.0 %copy.120 = f32[1,128,8,128]{3,2,1,0:T(8,128)} copy(f32[1,128,8,128]{1,3,2,0:T(8,128)} %bitcast.188) | data formatting | bytes 1048576 | tf_op jit(solution)/shard_map/squeeze | solution.py:71
  50.4 1.0 copy.118
  51.4 3.7 %slice.128 = f32[128,1023]{0,1:T(8,128)S(1)} reverse(f32[128,1023]{0,1:T(8,128)} %slice.152), dimensions={1} | reverse | bytes 1047552 | tf_op jit(solution)/shard_map/jit(_roll_static)/slice | solution.py:65
  55.2 1.5 %pad_maximum_fusion.12 = f32[1,128,1024]{1,2,0:T(8,128)} fusion(f32[1,128,1023]{1,2,0:T(8,128)S(1)} %bitcast.182, f32[1,128,1]{1,2,0:T(1,128)} %slice_bitcast_fusion.1), kind=kLoop, calls=%fused_computation.48 | loop fusion | flops 131072 | bytes 1048576 | tf_op jit(solution)/shard_map/jit(_roll_static)/concatenate | solution.py:65
  56.6 2.1 %copy.159 = f32[1,128,8,128]{3,2,1,0:T(8,128)} copy(f32[1,128,8,128]{1,3,2,0:T(8,128)} %bitcast.183) | data formatting | bytes 1048576 | tf_op jit(solution)/shard_map/jit(_roll_static)/concatenate | solution.py:65
  58.8 1.0 copy.126
  59.8 0.7 slice.133
  60.5 1.5 %pad_maximum_fusion.13 = f32[1,128,1024]{1,2,0:T(8,128)} fusion(f32[1,128,1023]{1,2,0:T(8,128)S(1)} %bitcast.184, f32[1,128,1]{1,2,0:T(1,128)} %slice_bitcast_fusion), kind=kLoop, calls=%fused_computation.49 | loop fusion | flops 131072 | bytes 1048576 | tf_op jit(solution)/shard_map/jit(_roll_static)/concatenate | solution.py:66
  62.1 2.1 %copy.160 = f32[1,128,8,128]{3,2,1,0:T(8,128)} copy(f32[1,128,8,128]{1,3,2,0:T(8,128)} %bitcast.185) | data formatting | bytes 1048576 | tf_op jit(solution)/shard_map/jit(_roll_static)/concatenate | solution.py:66
  64.2 1.6 %add_add_fusion = (f32[1,128,8,128]{3,2,1,0:T(8,128)S(1)}, f32[1,128,8,128]{3,2,1,0:T(8,128)S(1)}, f32[1,128,8,128]{3,2,1,0:T(8,128)S(1)}, f32[1,128,8,128]{3,2,1,0:T(8,128)S(1)}, f32[1,128,8,128]{3,2,1,0:T(8,128)S(1)}) fusion(f32[1,128,8,128]{3,2,1,0:T(8,128)S(1)} %copy.128, f32[1,128,8,128]{3,2,1,0:T(8,128)S(1)} %copy-done, ...), kind=kLoop, calls=%fused_computation.52 | loop fusion | flops 1966080 | bytes 5767168 | tf_op jit(solution)/shard_map/add | solution.py:80
  66.0 0.6 fusion.16
  66.7 0.6 fusion.17
  67.4 0.7 convolution_add_fusion.1
  68.0 0.9 add_bitcast_fusion
  68.9 0.9 fusion.8
  69.8 0.9 fusion.6
  70.7 0.9 fusion.1
  71.6 0.6 copy.191
  72.2 0.9 fusion
  73.1 0.6 copy.190
  74.5 1.5 %copy.143 = bf16[5,128,512]{1,0,2:T(8,128)(2,1)} copy(bf16[5,128,512]{1,2,0:T(8,128)(2,1)S(1)} %pad_maximum_fusion.11) | data formatting | bytes 1310720 | tf_op jit(solution)/shard_map/concatenate | solution.py:149
  76.0 3.6 %all-to-all-start.1 = ((bf16[5,128,512]{1,0,2:T(8,128)(2,1)}), bf16[5,128,512]{1,0,2:T(8,128)(2,1)S(1)}, u32[]{:S(2)}, u32[]{:S(2)}) async-start(bf16[5,128,512]{1,0,2:T(8,128)(2,1)} %copy.143), calls=%async_computation.1 | async-start | bytes 2097152 | tf_op jit(solution)/shard_map/all_to_all | solution.py:150
  79.8 15.3 %all_gather.6 = f32[3,512,3]{1,0,2:T(4,128)S(1)} all-gather(f32[3,128,3]{1,0,2:T(4,128)S(1)} %pad_maximum_fusion.14), channel_id=1, replica_groups=mesh['seq'=4,'chan'=8] {'seq'}, dimensions={1}, use_global_device_ids=true | all-gather | bytes 23040 | tf_op jit(solution)/shard_map/all_gather | solution.py:152
  95.1 0.6 copy.147
  95.7 5.0 %all-gather = f32[4,1,128]{2,1,0:T(1,128)S(1)} all-gather(f32[1,1,128]{2,1,0:T(1,128)S(1)} %bitcast.202), channel_id=1, replica_groups=mesh['seq'=4,'chan'=8] {'seq'}, dimensions={0}, use_global_device_ids=true | all-gather | bytes 2560 | tf_op jit(solution)/shard_map/all_gather | solution.py:153
  100.7 0.4 fusion.166
  101.1 0.3 slice.162
  101.4 0.8 copy.144
  102.2 1.0 copy.145
  103.2 0.8 copy.146
  104.0 0.6 copy.196
  (48 shorter events, 2.2 us)
Async XLA Ops:
  0.6 2.3 %copy-start.7 = (bf16[3,512,128]{2,1,0:T(8,128)(2,1)S(1)}, bf16[3,512,128]{2,1,0:T(8,128)(2,1)}, u32[]{:S(2)}) copy-start(bf16[3,512,128]{2,1,0:T(8,128)(2,1)} %param.5) | copy-start | bytes 1179652
  5.1 18.7 %all-to-all-start = ((bf16[5,512,128]{2,0,1:T(8,128)(2,1)}), bf16[5,512,128]{2,0,1:T(8,128)(2,1)S(1)}, u32[]{:S(2)}, u32[]{:S(2)}) async-start(bf16[5,512,128]{2,0,1:T(8,128)(2,1)} %pad_maximum_fusion), calls=%async_computation | async-start | bytes 2097152 | tf_op jit(solution)/shard_map/all_to_all | solution.py:132
  24.5 0.8 copy-start.1
  28.9 1.6 %copy-start.6 = (f32[128,512]{0,1:T(8,128)S(1)}, f32[128,512]{0,1:T(8,128)}, u32[]{:S(2)}) copy-start(f32[128,512]{0,1:T(8,128)} %get-tuple-element.23) | copy-start | bytes 786436
  33.2 2.0 %copy-start.3 = (f32[8,2,128,128]{3,0,2,1:T(8,128)S(1)}, f32[8,2,128,128]{3,0,2,1:T(8,128)}, u32[]{:S(2)}) copy-start(f32[8,2,128,128]{3,0,2,1:T(8,128)} %fusion.19) | copy-start | bytes 3145732
  33.2 2.0 %copy-start.9 = (f32[8,128]{1,0:T(8,128)S(1)}, f32[8,128]{1,0:T(8,128)}, u32[]{:S(2)}) copy-start(f32[8,128]{1,0:T(8,128)} %get-tuple-element.62) | copy-start | bytes 12292
  33.2 2.0 %copy-start.10 = (f32[8,128]{1,0:T(8,128)S(1)}, f32[8,128]{1,0:T(8,128)}, u32[]{:S(2)}) copy-start(f32[8,128]{1,0:T(8,128)} %get-tuple-element.63) | copy-start | bytes 12292
  56.6 3.1 %copy-start.4 = (f32[128,1023]{0,1:T(8,128)S(1)}, f32[128,1023]{0,1:T(8,128)}, u32[]{:S(2)}) copy-start(f32[128,1023]{0,1:T(8,128)} %slice.156) | copy-start | bytes 1571332
  60.5 3.7 %copy-start = (f32[1,128,8,128]{3,2,1,0:T(8,128)S(1)}, f32[1,128,8,128]{3,2,1,0:T(8,128)}, u32[]{:S(2)}) copy-start(f32[1,128,8,128]{3,2,1,0:T(8,128)} %copy.120) | copy-start | bytes 1572868
  62.1 2.1 %copy-start.5 = (f32[1,128,8,128]{3,2,1,0:T(8,128)S(1)}, f32[1,128,8,128]{3,2,1,0:T(8,128)}, u32[]{:S(2)}) copy-start(f32[1,128,8,128]{3,2,1,0:T(8,128)} %copy.118) | copy-start | bytes 1572868
  67.3 0.7 copy-start.8
  73.1 0.7 copy-start.12
  76.0 3.7 %copy-start.2 = (bf16[5,4,128,128]{2,3,1,0:T(8,128)(2,1)S(1)}, bf16[5,4,128,128]{2,3,1,0:T(8,128)(2,1)}, u32[]{:S(2)}) copy-start(bf16[5,4,128,128]{2,3,1,0:T(8,128)(2,1)} %copy-done.1) | copy-start | bytes 1966084
  76.0 24.7 %all-to-all-start.1 = ((bf16[5,128,512]{1,0,2:T(8,128)(2,1)}), bf16[5,128,512]{1,0,2:T(8,128)(2,1)S(1)}, u32[]{:S(2)}, u32[]{:S(2)}) async-start(bf16[5,128,512]{1,0,2:T(8,128)(2,1)} %copy.143), calls=%async_computation.1 | async-start | bytes 2097152 | tf_op jit(solution)/shard_map/all_to_all | solution.py:150
  79.6 16.0 %copy-start.11 = (f32[128]{0:T(128)S(1)}, f32[128]{0:T(128)}, u32[]{:S(2)}) copy-start(f32[128]{0:T(128)} %get-tuple-element.22) | copy-start | bytes 1540
where the time goes:
time: 105 us
  local copies, waits for them, and re-layouts  38.1 us (36%)
  blocking collectives  20.3 us (19%)
  matrix products  15.7 us (15%)
  waiting for transfers between devices  10.9 us (10%)
  other arithmetic  10.6 us (10%)
  starting transfers between devices  7.88 us (8%)
  between operations  1.1 us (1%)
    all_gather x1, blocking collectives, shards(): lax.all_gather(taps_grad, 'seq', axis=1, tiled=True)  15.3 us
    all_to_all x1, waiting for transfers between devices, shards(): lax.all_to_all(stacked, 'seq', split_axis=1, concat_axis=2, tiled=True)  10.9 us
    dot_general x8, matrix products, first_axis(): jnp.einsum('...ab,ak->...kb', operand, matrix, precision=lax.Precision.HIGH)  8.77 us
    dot_general x8, matrix products, last_axis(): jnp.einsum('...n,nk->...k', operand, matrix, precision=lax.Precision.HIGH)  6.96 us
    all_gather x1, blocking collectives, shards(): lax.all_gather(gain_grad, 'seq', axis=0, tiled=True)  5.05 us
    slice x2, local copies, waits for them, and re-layouts, spectral(): mirror_real = jnp.roll(jnp.flip(packed_real, -1), 1, -1)  4.57 us
    all_to_all x1, starting transfers between devices, shards(): lax.all_to_all(stacked, 'seq', split_axis=1, concat_axis=2, tiled=True)  4.24 us
    all_to_all x1, starting transfers between devices, shards(): lax.all_to_all(results, 'seq', split_axis=2, concat_axis=1, tiled=True)  3.65 us
  transfers between devices with their start and end apart: 2, of which 1 were waited for; matrix products, arithmetic and copies ran while one was open for 4% of the time, Pallas kernels for 0%

commit v1 on v0

--- a/solution.py
+++ b/solution.py
@@ -129,7 +129,10 @@
     margin = short_filters.shape[2] - 1
     local_gain = lax.dynamic_slice_in_dim(skip_gain, seq_index * per_group, per_group, 0)
     stacked = jnp.concatenate([features, cotangent[None], long_filter[None]], 0)
-    columns = lax.all_to_all(stacked, "seq", split_axis=1, concat_axis=2, tiled=True)
+    peers = lax.axis_size("seq")
+    pieces = jnp.stack(jnp.split(stacked, peers, axis=1), axis=0)
+    pieces = lax.all_to_all(pieces, "seq", split_axis=0, concat_axis=0)
+    columns = jnp.concatenate(pieces, axis=2)
     weights = lax.dynamic_slice_in_dim(short_filters, seq_index * per_group, per_group, 1)
     length = columns.shape[2]
     history = jnp.pad(columns[:3].astype(jnp.float32), ((0, 0), (0, 0), (margin, 0)))

time: 105 us -> 100 us (0.952)
  waiting for transfers between devices: 10.9 us -> 6.74 us
  other arithmetic: 10.6 us -> 8.34 us
    all_to_all x1, waiting for transfers between devices: 10.9 us -> 6.74 us  [shards(): pieces = lax.all_to_all(pieces, 'seq', split_axis=0, concat_axis=0)]
    unnamed x32 -> x39, local copies, waits for them, and re-layouts: 2.35 us -> 5.95 us
    broadcast_in_dim x2 -> x0, local copies, waits for them, and re-layouts: 2.27 us -> none  [shards(): stacked = jnp.concatenate([features, cotangent[None], long_filter[None]], 0)]
    concatenate x1, other arithmetic: 1.87 us -> 0.08 us  [shards(): stacked = jnp.concatenate([features, cotangent[None], long_filter[None]], 0)]
where the time goes in v1:
time: 100 us; the launch traced here: 99.1 us
  local copies, waits for them, and re-layouts  38.9 us (39%)
  blocking collectives  20.3 us (20%)
  matrix products  15.7 us (16%)
  other arithmetic  8.34 us (8%)
  starting transfers between devices  7.88 us (8%)
  waiting for transfers between devices  6.74 us (7%)
  between operations  1.13 us (1%)
    all_gather x1, blocking collectives, shards(): lax.all_gather(taps_grad, 'seq', axis=1, tiled=True)  15.3 us
    dot_general x8, matrix products, first_axis(): jnp.einsum('...ab,ak->...kb', operand, matrix, precision=lax.Precision.HIGH)  8.76 us
    dot_general x8, matrix products, last_axis(): jnp.einsum('...n,nk->...k', operand, matrix, precision=lax.Precision.HIGH)  6.96 us
    all_to_all x1, waiting for transfers between devices, shards(): pieces = lax.all_to_all(pieces, 'seq', split_axis=0, concat_axis=0)  6.74 us
    unnamed x39, local copies, waits for them, and re-layouts  5.95 us
    all_gather x1, blocking collectives, shards(): lax.all_gather(gain_grad, 'seq', axis=0, tiled=True)  5.05 us
    slice x2, local copies, waits for them, and re-layouts, spectral(): mirror_real = jnp.roll(jnp.flip(packed_real, -1), 1, -1)  4.55 us
    all_to_all x1, starting transfers between devices, shards(): pieces = lax.all_to_all(pieces, 'seq', split_axis=0, concat_axis=0)  4.24 us
  transfers between devices with their start and end apart: 2, of which 1 were waited for; matrix products, arithmetic and copies ran while one was open for 4% of the time, Pallas kernels for 0%

profile of v1, /device:TPU:0, one launch (start us, length us, event | category | flops | bytes accessed | tf_op | source)
XLA Modules:
  0.0 99.1 jit_solution(103293544028999403)
XLA Ops:
  0.7 1.1 %copy.65 = bf16[512,128]{0,1:T(8,128)(2,1)S(1)} copy(bf16[512,128]{1,0:T(8,128)(2,1)} %param.7) | data formatting | bytes 262144 | tf_op args[2]
  2.3 0.9 pad_maximum_fusion.11
  3.3 4.2 %all-to-all-start = ((bf16[4,5,128,128]{2,3,1,0:T(8,128)(2,1)}), bf16[4,5,128,128]{2,3,1,0:T(8,128)(2,1)S(1)}, u32[]{:S(2)}, u32[]{:S(2)}) async-start(bf16[4,5,128,128]{2,3,1,0:T(8,128)(2,1)} %pad_maximum_fusion.11), calls=%async_computation | async-start | bytes 1310720 | tf_op jit(solution)/shard_map/all_to_all | solution.py:134
  7.5 0.9 constant_dynamic-slice_fusion.1
  8.4 1.3 %dynamic_slice.7 = f32[128]{0:T(128)} dynamic-slice(f32[512]{0:T(512)} %param.9, s32[]{:T(128)S(6)} %select_n.84), dynamic_slice_sizes={128} | dynamic-slice | bytes 1028 | tf_op jit(solution)/shard_map/dynamic_slice | solution.py:130
  9.7 0.7 multiply_sine_fusion.7
  10.3 0.6 multiply_sine_fusion.6
  11.0 6.7 %all-to-all-done = bf16[4,5,128,128]{2,3,1,0:T(8,128)(2,1)S(1)} async-done(((bf16[4,5,128,128]{2,3,1,0:T(8,128)(2,1)}), bf16[4,5,128,128]{2,3,1,0:T(8,128)(2,1)S(1)}, u32[]{:S(2)}, u32[]{:S(2)}) %all-to-all-start) | async-done | bytes 655392 | tf_op jit(solution)/shard_map/all_to_all | solution.py:134
  17.9 0.7 copy-done.1
  19.1 1.3 %multiply_reduce_fusion.2 = (f32[128]{0:T(128)}, f32[128,512]{0,1:T(8,128)}, bf16[1,128,512]{1,2,0:T(8,128)(2,1)S(1)}) fusion(f32[3,128,512]{1,2,0:T(8,128)S(1)} %multiply_add_fusion, f32[1,128,4,128]{1,3,2,0:T(8,128)S(1)} %get-tuple-element.46), kind=kLoop, calls=%fused_computation.81 | loop fusion | flops 524160 | bytes 1442304 | tf_op jit(solution)/shard_map/reduce_sum | solution.py:151
  20.7 1.6 %fusion.18 = f32[8,2,128,128]{3,0,2,1:T(8,128)} fusion(f32[1,128,8,128]{3,2,1,0:T(8,128)S(1)} %copy.115, f32[1,128,8,128]{3,2,1,0:T(8,128)S(1)} %copy.114), kind=kOutput, calls=%fused_computation.35 | convolution fusion | flops 12845952 | bytes 2097152 | tf_op jit(solution)/shard_map/...ab,ak->...kb/dot_general | solution.py:24
  22.3 1.6 %fusion.19 = f32[8,2,128,128]{3,0,2,1:T(8,128)} fusion(f32[1,128,8,128]{3,2,1,0:T(8,128)S(1)} %copy.115, f32[1,128,8,128]{3,2,1,0:T(8,128)S(1)} %copy.114), kind=kOutput, calls=%fused_computation.36 | convolution fusion | flops 12845952 | bytes 2097152 | tf_op jit(solution)/shard_map/...ab,ak->...kb/dot_general | solution.py:24
  23.9 1.1 %stack.78 = f32[2,128,1024]{1,2,0:T(8,128)} pad(f32[1,128,1024]{1,2,0:T(8,128)S(1)} %pad_bitcast_fusion, f32[]{:T(128)} %constant.67.clone.1), padding=0_1x0_0x0_0 | pad | bytes 1572868 | tf_op jit(solution)/shard_map/stack | solution.py:59
  25.0 1.6 %copy.116 = f32[2,128,8,128]{3,2,1,0:T(8,128)S(1)} copy(f32[2,128,8,128]{1,3,2,0:T(8,128)} %bitcast.181) | data formatting | bytes 2097152 | tf_op jit(solution)/shard_map/reshape | solution.py:38
  26.6 1.9 %convolution_add_fusion.3 = f32[8,2,128,128]{3,0,2,1:T(8,128)S(1)} fusion(f32[8,2,128,128]{3,0,2,1:T(8,128)} %fusion.18, f32[2,128,8,128]{3,2,1,0:T(8,128)S(1)} %copy.116), kind=kOutput, calls=%fused_computation.10 | convolution fusion | flops 12845952 | bytes 3145728 | tf_op jit(solution)/shard_map/...ab,ak->...kb/dot_general | solution.py:24
  28.6 0.8 add_bitcast_fusion.1
  29.4 0.9 fusion.12
  30.3 0.9 fusion.14
  31.1 0.9 fusion.3
  32.0 0.9 fusion.168
  32.9 0.3 copy.153
  33.2 0.8 slice.152
  34.1 0.5 slice_bitcast_fusion.5
  34.6 0.9 fusion.2
  35.5 0.3 copy.152
  35.9 0.8 slice.156
  36.7 0.5 slice_bitcast_fusion.4
  37.2 1.1 %copy.85 = f32[1,128,128,8]{1,3,2,0:T(8,128)} copy(f32[1,128,128,8]{1,2,3,0:T(8,128)S(1)} %get-tuple-element.40) | data formatting | bytes 1048576 | tf_op jit(solution)/shard_map/slice | solution.py:72
  38.3 1.3 %copy.86 = f32[1,128,8,128]{3,2,1,0:T(8,128)S(1)} copy(f32[1,128,8,128]{1,3,2,0:T(8,128)} %bitcast.191) | data formatting | bytes 1048576 | tf_op jit(solution)/shard_map/squeeze | solution.py:72
  39.6 2.1 %copy.77 = f32[1,128,128,8]{1,3,2,0:T(8,128)} copy(f32[1,128,128,8]{1,2,3,0:T(8,128)} %get-tuple-element.42) | data formatting | bytes 1048576 | tf_op jit(solution)/shard_map/slice | solution.py:71
  41.7 2.1 %copy.78 = f32[1,128,8,128]{3,2,1,0:T(8,128)} copy(f32[1,128,8,128]{1,3,2,0:T(8,128)} %bitcast.192) | data formatting | bytes 1048576 | tf_op jit(solution)/shard_map/squeeze | solution.py:71
  43.8 1.0 %copy.76 = f32[1,128,8,128]{3,2,1,0:T(8,128)} copy(f32[1,128,8,128]{1,3,2,0:T(8,128)S(1)} %bitcast.172) | data formatting | bytes 1048576 | tf_op jit(solution)/shard_map/squeeze | solution.py:63
  44.8 3.7 %slice.128 = f32[128,1023]{0,1:T(8,128)S(1)} reverse(f32[128,1023]{0,1:T(8,128)} %slice.152), dimensions={1} | reverse | bytes 1047552 | tf_op jit(solution)/shard_map/jit(_roll_static)/slice | solution.py:65
  48.5 0.6 copy-done.13
  49.2 0.8 pad_maximum_fusion.13
  50.0 2.0 %copy.117 = f32[1,128,8,128]{3,2,1,0:T(8,128)} copy(f32[1,128,8,128]{1,3,2,0:T(8,128)} %bitcast.187) | data formatting | bytes 1048576 | tf_op jit(solution)/shard_map/jit(_roll_static)/concatenate | solution.py:65
  52.0 1.0 %copy.84 = f32[1,128,8,128]{3,2,1,0:T(8,128)} copy(f32[1,128,8,128]{1,3,2,0:T(8,128)S(1)} %bitcast.175) | data formatting | bytes 1048576 | tf_op jit(solution)/shard_map/squeeze | solution.py:64
  53.1 0.7 slice.133
  53.8 0.6 copy-done.14
  54.4 0.8 pad_maximum_fusion.14
  55.3 2.1 %copy.118 = f32[1,128,8,128]{3,2,1,0:T(8,128)} copy(f32[1,128,8,128]{1,3,2,0:T(8,128)} %bitcast.189) | data formatting | bytes 1048576 | tf_op jit(solution)/shard_map/jit(_roll_static)/concatenate | solution.py:66
  57.4 1.6 %add_add_fusion = (f32[1,128,8,128]{3,2,1,0:T(8,128)S(1)}, f32[1,128,8,128]{3,2,1,0:T(8,128)S(1)}, f32[1,128,8,128]{3,2,1,0:T(8,128)S(1)}, f32[1,128,8,128]{3,2,1,0:T(8,128)S(1)}, f32[1,128,8,128]{3,2,1,0:T(8,128)S(1)}) fusion(f32[1,128,8,128]{3,2,1,0:T(8,128)S(1)} %copy.86, f32[1,128,8,128]{3,2,1,0:T(8,128)S(1)} %copy-done, ...), kind=kLoop, calls=%fused_computation.53 | loop fusion | flops 1966080 | bytes 5767168 | tf_op jit(solution)/shard_map/add | solution.py:80
  59.3 0.6 fusion.16
  59.9 0.6 fusion.17
  60.6 0.7 convolution_add_fusion.1
  61.3 0.9 add_bitcast_fusion
  62.2 0.9 fusion.8
  63.1 0.9 fusion.6
  64.0 0.9 fusion.1
  64.8 0.6 copy.149
  65.4 0.9 fusion
  66.3 0.6 copy.148
  67.0 0.6 copy-done.15
  68.4 1.5 %copy.101 = bf16[5,128,512]{1,0,2:T(8,128)(2,1)} copy(bf16[5,128,512]{1,2,0:T(8,128)(2,1)S(1)} %pad_maximum_fusion.12) | data formatting | bytes 1310720 | tf_op jit(solution)/shard_map/concatenate | solution.py:152
  69.8 3.6 %all-to-all-start.1 = ((bf16[5,128,512]{1,0,2:T(8,128)(2,1)}), bf16[5,128,512]{1,0,2:T(8,128)(2,1)S(1)}, u32[]{:S(2)}, u32[]{:S(2)}) async-start(bf16[5,128,512]{1,0,2:T(8,128)(2,1)} %copy.101), calls=%async_computation.1 | async-start | bytes 2097152 | tf_op jit(solution)/shard_map/all_to_all | solution.py:153
  73.6 15.3 %all_gather.6 = f32[3,512,3]{1,0,2:T(4,128)S(1)} all-gather(f32[3,128,3]{1,0,2:T(4,128)S(1)} %pad_maximum_fusion.15), channel_id=1, replica_groups=mesh['seq'=4,'chan'=8] {'seq'}, dimensions={1}, use_global_device_ids=true | all-gather | bytes 23040 | tf_op jit(solution)/shard_map/all_gather | solution.py:155
  88.9 0.6 copy.105
  89.5 0.7 copy-done.12
  90.2 5.0 %all-gather = f32[4,1,128]{2,1,0:T(1,128)S(1)} all-gather(f32[1,1,128]{2,1,0:T(1,128)S(1)} %bitcast.207), channel_id=1, replica_groups=mesh['seq'=4,'chan'=8] {'seq'}, dimensions={0}, use_global_device_ids=true | all-gather | bytes 2560 | tf_op jit(solution)/shard_map/all_gather | solution.py:156
  95.2 0.4 fusion.166
  95.9 0.8 copy.102
  96.7 1.0 %copy.103 = bf16[3,4,128,128]{3,2,1,0:T(8,128)(2,1)} copy(bf16[3,4,128,128]{2,0,3,1:T(4,128)(2,1)S(1)} %slice.162) | data formatting | bytes 786432 | tf_op jit(solution)/shard_map/slice | solution.py:158
  97.7 0.8 copy.104
  98.5 0.6 copy.155
  (55 shorter events, 3.0 us)
Async XLA Ops:
  0.6 1.1 %copy-start.8 = (bf16[512,128]{1,0:T(8,128)(2,1)S(1)}, bf16[512,128]{1,0:T(8,128)(2,1)}, u32[]{:S(2)}) copy-start(bf16[512,128]{1,0:T(8,128)(2,1)} %param.6) | copy-start | bytes 393220
  0.6 1.2 %copy-start.7 = (bf16[3,512,128]{2,1,0:T(8,128)(2,1)S(1)}, bf16[3,512,128]{2,1,0:T(8,128)(2,1)}, u32[]{:S(2)}) copy-start(bf16[3,512,128]{2,1,0:T(8,128)(2,1)} %param.5) | copy-start | bytes 1179652
  3.3 14.5 %all-to-all-start = ((bf16[4,5,128,128]{2,3,1,0:T(8,128)(2,1)}), bf16[4,5,128,128]{2,3,1,0:T(8,128)(2,1)S(1)}, u32[]{:S(2)}, u32[]{:S(2)}) async-start(bf16[4,5,128,128]{2,3,1,0:T(8,128)(2,1)} %pad_maximum_fusion.11), calls=%async_computation | async-start | bytes 1310720 | tf_op jit(solution)/shard_map/all_to_all | solution.py:134
  17.8 0.8 copy-start.1
  22.3 1.6 %copy-start.6 = (f32[128,512]{0,1:T(8,128)S(1)}, f32[128,512]{0,1:T(8,128)}, u32[]{:S(2)}) copy-start(f32[128,512]{0,1:T(8,128)} %get-tuple-element.18) | copy-start | bytes 786436
  26.6 2.0 %copy-start.3 = (f32[8,2,128,128]{3,0,2,1:T(8,128)S(1)}, f32[8,2,128,128]{3,0,2,1:T(8,128)}, u32[]{:S(2)}) copy-start(f32[8,2,128,128]{3,0,2,1:T(8,128)} %fusion.19) | copy-start | bytes 3145732
  26.6 2.0 %copy-start.10 = (f32[8,128]{1,0:T(8,128)S(1)}, f32[8,128]{1,0:T(8,128)}, u32[]{:S(2)}) copy-start(f32[8,128]{1,0:T(8,128)} %get-tuple-element.61) | copy-start | bytes 12292
  26.6 2.0 %copy-start.11 = (f32[8,128]{1,0:T(8,128)S(1)}, f32[8,128]{1,0:T(8,128)}, u32[]{:S(2)}) copy-start(f32[8,128]{1,0:T(8,128)} %get-tuple-element.62) | copy-start | bytes 12292
  48.5 0.7 copy-start.13
  52.0 1.0 %copy-start.4 = (f32[128,1023]{0,1:T(8,128)S(1)}, f32[128,1023]{0,1:T(8,128)}, u32[]{:S(2)}) copy-start(f32[128,1023]{0,1:T(8,128)} %slice.156) | copy-start | bytes 1571332
  53.8 0.7 copy-start.14
  55.3 2.1 %copy-start = (f32[1,128,8,128]{3,2,1,0:T(8,128)S(1)}, f32[1,128,8,128]{3,2,1,0:T(8,128)}, u32[]{:S(2)}) copy-start(f32[1,128,8,128]{3,2,1,0:T(8,128)} %copy.78) | copy-start | bytes 1572868
  55.3 2.1 %copy-start.5 = (f32[1,128,8,128]{3,2,1,0:T(8,128)S(1)}, f32[1,128,8,128]{3,2,1,0:T(8,128)}, u32[]{:S(2)}) copy-start(f32[1,128,8,128]{3,2,1,0:T(8,128)} %copy.76) | copy-start | bytes 1572868
  60.6 0.7 copy-start.9
  66.9 0.6 copy-start.15
  69.8 3.7 %copy-start.2 = (bf16[4,5,128,128]{2,3,0,1:T(8,128)(2,1)S(1)}, bf16[4,5,128,128]{2,3,0,1:T(8,128)(2,1)}, u32[]{:S(2)}) copy-start(bf16[4,5,128,128]{2,3,0,1:T(8,128)(2,1)} %copy-done.1) | copy-start | bytes 1966084
  69.8 25.4 %all-to-all-start.1 = ((bf16[5,128,512]{1,0,2:T(8,128)(2,1)}), bf16[5,128,512]{1,0,2:T(8,128)(2,1)S(1)}, u32[]{:S(2)}, u32[]{:S(2)}) async-start(bf16[5,128,512]{1,0,2:T(8,128)(2,1)} %copy.101), calls=%async_computation.1 | async-start | bytes 2097152 | tf_op jit(solution)/shard_map/all_to_all | solution.py:153
  89.5 0.7 copy-start.12
